TPU v7x, 256 devices: a whole 4x4x8 slice. The times are simulated.
256 devices in a mesh: dp: 4 (over y), seq: 16 (over z, core), mp: 4 (over x).
Axes of the slice: x: 4, y: 4, z: 8, core: 2. Of those that a mesh axis runs over, the one named last changes fastest.
Arguments:
- q_self: bfloat16 [4, 1024, 4096], P('dp', 'seq', 'mp'), may hold values from -12 to 12
- k_self: bfloat16 [4, 1024, 4096], P('dp', 'seq', 'mp'), may hold values from -3 to 3
- v_self: bfloat16 [4, 1024, 4096], P('dp', 'seq', 'mp'), may hold values from -0.75 to 0.75
- out_grad_self: bfloat16 [4, 1024, 4096], P('dp', 'seq', 'mp'), may hold values from -6 to 6
- q_cross: bfloat16 [4, 1024, 4096], P('dp', 'seq', 'mp'), may hold values from -12 to 12
- k_cross: bfloat16 [4, 2048, 4096], P('dp', 'seq', 'mp'), may hold values from -3 to 3
- v_cross: bfloat16 [4, 2048, 4096], P('dp', 'seq', 'mp'), may hold values from -0.75 to 0.75
- out_grad_cross: bfloat16 [4, 1024, 4096], P('dp', 'seq', 'mp'), may hold values from -8 to 8
- dec_lengths: int32 [4, 16], P('dp'), may hold values from 1 to 640, as said below
- enc_lengths: int32 [4, 16], P('dp'), may hold values from 1 to 1280, as said below
- rel_bias: float32 [32, 64], P(None, 'mp'), may hold values from -4 to 4
Outputs:
- grad_q_self: bfloat16 [4, 1024, 4096], P('dp', 'seq', 'mp')
- grad_k_self: bfloat16 [4, 1024, 4096], P('dp', 'seq', 'mp')
- grad_v_self: bfloat16 [4, 1024, 4096], P('dp', 'seq', 'mp')
- grad_q_cross: bfloat16 [4, 1024, 4096], P('dp', 'seq', 'mp')
- grad_k_cross: bfloat16 [4, 2048, 4096], P('dp', 'seq', 'mp')
- grad_v_cross: bfloat16 [4, 2048, 4096], P('dp', 'seq', 'mp')
- bias_grad: float32 [32, 64], P(None, 'mp')
Inputs may be any that keep to these rules, and one draw needn't show every extreme that they name: `dec_lengths`: row p lists the decoder lengths of the 16 examples of pack p in order; they sum to 1024 and the largest is exactly 640. `enc_lengths`: row p lists the encoder lengths of the same 16 examples in the same order; they sum to 2048. The example with 640 decoder rows has exactly 1280 encoder rows; every other example has at least as many encoder rows as decoder rows and at most three times as many.
All inputs are finite; a program needn't handle non-finite values.
Results may differ from a plain program's by a relative error of at most 0.039.
Values may be sent and summed in bfloat16 or wider, within the bound.
A program may use at most 128 MiB of HBM per device.

v0:
```python
import math
import jax
import jax.numpy as jnp
from jax import lax
from jax.sharding import PartitionSpec as P

HEAD_DIM = 64
BUCKETS = 32
DISTANCE = 128


def bucket_of(distances):
    exact_count = BUCKETS // 2
    bucketed = jnp.full(distances.shape, exact_count, jnp.int32)
    for level_index in range(1, BUCKETS - exact_count):
        threshold = math.ceil(
            exact_count * (DISTANCE / exact_count) ** (level_index / (BUCKETS - exact_count))
        )
        bucketed = bucketed + (distances >= threshold).astype(jnp.int32)
    return jnp.where(distances < exact_count, distances, bucketed)


def example_ids(total_rows, lengths):
    segment_ends = jnp.cumsum(lengths)
    positions = jnp.arange(total_rows, dtype=jnp.int32)
    return jnp.sum((positions[:, None] >= segment_ends[None, :]).astype(jnp.int32), axis=1)


def distance_table(rel_bias, offset_base, table_span):
    distances = offset_base + jnp.arange(table_span, dtype=jnp.int32)
    buckets = bucket_of(jnp.maximum(distances, 0))
    one_hot = (buckets[None, :] == jnp.arange(rel_bias.shape[0], dtype=jnp.int32)[:, None]).astype(
        jnp.float32
    )
    bias_table = jnp.einsum("bh,bl->hl", rel_bias, one_hot, precision=lax.Precision.HIGHEST)
    return (one_hot, bias_table)


def spread(bias_table, row_count, col_count):
    full_span = row_count + col_count - 1
    leading = bias_table.shape[:-1]
    tiled_rows = jnp.broadcast_to(bias_table[..., None, :], leading + (row_count, full_span))
    flat_rows = tiled_rows.reshape(leading + (row_count * full_span,))
    flat_rows = jnp.pad(flat_rows, [(0, 0)] * len(leading) + [(0, row_count)])
    skewed = flat_rows.reshape(leading + (row_count, full_span + 1))[..., :col_count]
    return skewed[..., ::-1]


def collapse(matrix, row_count, col_count):
    full_span = row_count + col_count - 1
    leading = matrix.shape[:-2]
    flipped = matrix[..., ::-1]
    padded = jnp.pad(flipped, [(0, 0)] * len(leading) + [(0, 0), (0, row_count)])
    flat_rows = padded.reshape(leading + (row_count * (full_span + 1),))[
        ..., : row_count * full_span
    ]
    return jnp.sum(flat_rows.reshape(leading + (row_count, full_span)), axis=-2)


def shard_group(shard_count, row_count):
    group_size = 1
    while group_size < shard_count and (
        shard_count % group_size != 0 or group_size * row_count < 384
    ):
        group_size += 1
    return group_size


def query_side(
    queries,
    out_grads,
    all_keys,
    all_values,
    key_ids,
    query_ids,
    query_start,
    rel_bias,
    block_rows,
    causal,
):
    row_count, head_count, head_size = queries.shape
    block_count = all_keys.shape[0] // block_rows
    query_pos = query_start + jnp.arange(row_count, dtype=jnp.int32)
    block_ids = jnp.arange(block_count, dtype=jnp.int32)

    def scores_of(block_id):
        key_first = block_id * block_rows
        key_block = lax.dynamic_slice_in_dim(all_keys, key_first, block_rows, 0)
        key_block_ids = lax.dynamic_slice_in_dim(key_ids, key_first, block_rows, 0)
        scores = jnp.einsum("thd,uhd->htu", queries, key_block, preferred_element_type=jnp.float32)
        allowed = query_ids[:, None] == key_block_ids[None, :]
        one_hot = jnp.zeros((1, 1), jnp.float32)
        if causal:
            key_pos = key_first + jnp.arange(block_rows, dtype=jnp.int32)
            allowed = allowed & (query_pos[:, None] >= key_pos[None, :])
            one_hot, bias_table = distance_table(
                rel_bias, query_start - key_first - (block_rows - 1), row_count + block_rows - 1
            )
            scores = scores + spread(bias_table, row_count, block_rows)
        return (jnp.where(allowed[None], scores, -1e30), one_hot)

    def stat_step(running, block_id):
        row_high, total_sum = running
        scores, unused_hot = scores_of(block_id)
        new_high = jnp.maximum(row_high, jnp.max(scores, axis=2))
        total_sum = total_sum * jnp.exp(row_high - new_high) + jnp.sum(
            jnp.exp(scores - new_high[:, :, None]), axis=2
        )
        return ((new_high, total_sum), None)

    start_state = (
        jnp.full((head_count, row_count), -1e30, jnp.float32),
        jnp.zeros((head_count, row_count), jnp.float32),
    )
    (row_high, total_sum), unused_stats = lax.scan(stat_step, start_state, block_ids)

    def weights_of(scores):
        return jnp.exp(scores - row_high[:, :, None]) / total_sum[:, :, None]

    def out_step(summed, block_id):
        scores, unused_hot = scores_of(block_id)
        narrow_weights = weights_of(scores).astype(jnp.bfloat16)
        value_block = lax.dynamic_slice_in_dim(all_values, block_id * block_rows, block_rows, 0)
        return (
            summed
            + jnp.einsum(
                "htu,uhd->thd", narrow_weights, value_block, preferred_element_type=jnp.float32
            ),
            None,
        )

    summed, unused_outs = lax.scan(
        out_step, jnp.zeros((row_count, head_count, head_size), jnp.float32), block_ids
    )
    outputs = summed.astype(jnp.bfloat16)
    row_delta = jnp.einsum("thd,thd->ht", out_grads, outputs, preferred_element_type=jnp.float32)

    def grad_step(running, block_id):
        query_grad, bias_grad_sum = running
        scores, one_hot = scores_of(block_id)
        weights = weights_of(scores)
        narrow_weights = weights.astype(jnp.bfloat16)
        key_block = lax.dynamic_slice_in_dim(all_keys, block_id * block_rows, block_rows, 0)
        value_block = lax.dynamic_slice_in_dim(all_values, block_id * block_rows, block_rows, 0)
        weight_grads = jnp.einsum(
            "thd,uhd->htu", out_grads, value_block, preferred_element_type=jnp.float32
        )
        score_grads = weights * (weight_grads - row_delta[:, :, None])
        narrow_grads = score_grads.astype(jnp.bfloat16)
        query_grad = query_grad + jnp.einsum(
            "htu,uhd->thd", narrow_grads, key_block, preferred_element_type=jnp.float32
        )
        if causal:
            bias_grad_sum = bias_grad_sum + jnp.einsum(
                "hl,bl->bh",
                collapse(score_grads, row_count, block_rows),
                one_hot,
                precision=lax.Precision.HIGHEST,
            )
        key_term = jnp.einsum(
            "htu,thd->uhd", narrow_grads, queries, preferred_element_type=jnp.float32
        )
        value_term = jnp.einsum(
            "htu,thd->uhd", narrow_weights, out_grads, preferred_element_type=jnp.float32
        )
        grad_term = jnp.concatenate(
            [
                key_term.reshape(block_rows, head_count * head_size),
                value_term.reshape(block_rows, head_count * head_size),
            ],
            axis=1,
        ).astype(jnp.bfloat16)
        return ((query_grad, bias_grad_sum), grad_term)

    grad_state = (
        jnp.zeros((row_count, head_count, head_size), jnp.float32),
        jnp.zeros((rel_bias.shape[0], head_count), jnp.float32),
    )
    (query_grad, bias_grad_sum), grad_terms = lax.scan(grad_step, grad_state, block_ids)
    grad_terms = grad_terms.reshape(block_count * block_rows, 2 * head_count * head_size)
    query_grad = query_grad.astype(jnp.bfloat16).reshape(row_count, head_count * head_size)
    return (query_grad, grad_terms, bias_grad_sum, (row_high, total_sum, row_delta))


def on_device(
    q_self,
    k_self,
    v_self,
    out_grad_self,
    q_cross,
    k_cross,
    v_cross,
    out_grad_cross,
    dec_lengths,
    enc_lengths,
    rel_bias,
):
    seq_count = lax.axis_size("seq")
    seq_place = lax.axis_index("seq")
    dec_rows = q_self.shape[1]
    enc_rows = k_cross.shape[1]
    feature_count = q_self.shape[2]
    head_count = feature_count // HEAD_DIM
    dec_total = dec_rows * seq_count
    enc_total = enc_rows * seq_count
    dec_start = seq_place * dec_rows
    dec_ids = example_ids(dec_total, dec_lengths[0])
    enc_ids = example_ids(enc_total, enc_lengths[0])
    my_dec_ids = lax.dynamic_slice_in_dim(dec_ids, dec_start, dec_rows, 0)

    def split_heads(tensor):
        return tensor.reshape(tensor.shape[0] * tensor.shape[1], head_count, HEAD_DIM)

    gathered = (
        lax.all_gather(k_self, "seq", axis=1, tiled=True),
        lax.all_gather(v_self, "seq", axis=1, tiled=True),
        lax.all_gather(k_cross, "seq", axis=1, tiled=True),
        lax.all_gather(v_cross, "seq", axis=1, tiled=True),
    )
    self_group = shard_group(seq_count, dec_rows)
    cross_group = shard_group(seq_count, enc_rows)
    self_dq, self_terms, self_bias, self_stats = query_side(
        split_heads(q_self),
        split_heads(out_grad_self),
        split_heads(gathered[0]),
        split_heads(gathered[1]),
        dec_ids,
        my_dec_ids,
        dec_start,
        rel_bias,
        self_group * dec_rows,
        True,
    )
    cross_dq, cross_terms, unused_bias, cross_stats = query_side(
        split_heads(q_cross),
        split_heads(out_grad_cross),
        split_heads(gathered[2]),
        split_heads(gathered[3]),
        enc_ids,
        my_dec_ids,
        dec_start,
        rel_bias,
        cross_group * enc_rows,
        False,
    )
    self_sums = lax.psum_scatter(
        self_terms.astype(jnp.float32).astype(jnp.bfloat16), "seq", scatter_dimension=0, tiled=True
    ).astype(jnp.float32)
    cross_sums = lax.psum_scatter(
        cross_terms.astype(jnp.float32).astype(jnp.bfloat16), "seq", scatter_dimension=0, tiled=True
    ).astype(jnp.float32)
    self_key_grad = self_sums[:, :feature_count]
    self_value_grad = self_sums[:, feature_count:]
    cross_key_grad = cross_sums[:, :feature_count]
    cross_value_grad = cross_sums[:, feature_count:]
    bias_total = lax.psum(self_bias, ("dp", "seq"))
    bias_grad = bias_total * (1.0 / math.sqrt(lax.axis_size("dp") * dec_total))
    return (
        self_dq.reshape(1, dec_rows, feature_count),
        self_key_grad.reshape(1, dec_rows, feature_count).astype(jnp.bfloat16),
        self_value_grad.reshape(1, dec_rows, feature_count).astype(jnp.bfloat16),
        cross_dq.reshape(1, dec_rows, feature_count),
        cross_key_grad.reshape(1, enc_rows, feature_count).astype(jnp.bfloat16),
        cross_value_grad.reshape(1, enc_rows, feature_count).astype(jnp.bfloat16),
        bias_grad,
    )


def solution(mesh):
    return jax.shard_map(
        on_device,
        mesh=mesh,
        in_specs=(
            P("dp", "seq", "mp"),
            P("dp", "seq", "mp"),
            P("dp", "seq", "mp"),
            P("dp", "seq", "mp"),
            P("dp", "seq", "mp"),
            P("dp", "seq", "mp"),
            P("dp", "seq", "mp"),
            P("dp", "seq", "mp"),
            P("dp", None),
            P("dp", None),
            P(None, "mp"),
        ),
        out_specs=(
            P("dp", "seq", "mp"),
            P("dp", "seq", "mp"),
            P("dp", "seq", "mp"),
            P("dp", "seq", "mp"),
            P("dp", "seq", "mp"),
            P("dp", "seq", "mp"),
            P(None, "mp"),
        ),
        check_vma=False,
    )
```

profile of v0, /device:TPU:2, one launch (start us, length us, event | category | flops | bytes accessed | tf_op | source)
XLA Modules:
  0.0 455.4 jit_solution(5825784003897655049)
XLA Ops:
  17.9 34.6 %all-gather.5.cloned.1.call-done = bf16[1,1024,1024]{2,1,0:T(8,128)(2,1)} async-done(((bf16[1,64,1024]{2,1,0:T(8,128)(2,1)}), bf16[1,1024,1024]{2,1,0:T(8,128)(2,1)}) %all-gather.5.cloned.1.call-update) | async-done | bytes 2097168 | tf_op jit(solution)/shard_map/all_gather | solution.py:215
  52.6 3.9 copy.70
  56.5 31.9 %while.91 = (s32[]{:T(128)}, f32[16,64]{1,0:T(8,128)S(1)}, f32[16,64]{1,0:T(8,128)S(1)}, s32[64]{0:T(128)S(1)}, s32[2]{0:T(128)S(1)}, /*index=5*/s32[1024]{0:T(1...) while((s32[]{:T(128)}, f32[16,64]{1,0:T(8,128)S(1)}, ...), condition=%wide.region_5.6_spmd.clone.clone.clone, body=%wide.region_2.0_spmd.clone.clone.clone.sunk | while | flops 73413688 | bytes 34665884 | solution.py:115
  88.4 4.1 all-gather.7.cloned.1.call-done
  92.5 3.9 copy.74
  96.4 34.2 %while.92 = (s32[]{:T(128)}, f32[64,16,64]{0,2,1:T(8,128)}, s32[2]{0:T(128)S(1)}, bf16[1024,16,64]{0,2,1:T(8,128)(2,1)}, s32[64]{0:T(128)S(1)}, /*index=5*/s32[1...) while((s32[]{:T(128)}, f32[64,16,64]{0,2,1:T(8,128)}, ...), condition=%wide.region_7.8_spmd.clone.clone.clone, body=%wide.region_6.7_spmd.clone.clone.clone.sunk | while | flops 140648496 | bytes 34098144 | solution.py:132
  109.2 3.4 fusion.213
  126.3 3.4 fusion.213
  131.7 80.7 %while.93 = (s32[]{:T(128)}, f32[64,16,64]{0,2,1:T(8,128)}, f32[32,16]{0,1:T(8,128)S(1)}, bf16[2,512,2048]{2,1,0:T(8,128)(2,1)}, s32[2]{0:T(128)S(1)}, /*index=5...) while((s32[]{:T(128)}, f32[64,16,64]{0,2,1:T(8,128)}, ...), condition=%wide.region_10.11_spmd.clone.clone.clone, body=%wide.region_8.10_spmd.clone.clone.clone.sunk | while | flops 353446976 | bytes 101543680 | solution.py:179
  164.8 3.7 reshape.726
  168.9 3.3 constant_dynamic-update-slice_fusion.5
  184.9 2.7 fusion.226
  205.1 3.7 reshape.726
  209.2 3.3 constant_dynamic-update-slice_fusion.5
  212.6 6.7 %copy.79 = bf16[1,2048,1024]{1,2,0:T(8,128)(2,1)} copy(bf16[1,2048,1024]{2,1,0:T(8,128)(2,1)} %all-gather.9.cloned.1.call-done) | data formatting | bytes 8388608 | tf_op jit(solution)/shard_map/all_gather | solution.py:217
  219.4 15.2 %while.88 = (s32[]{:T(128)}, f32[16,64]{1,0:T(8,128)S(1)}, f32[16,64]{1,0:T(8,128)S(1)}, s32[64]{0:T(128)S(1)}, s32[4]{0:T(128)S(1)}, /*index=5*/s32[2048]{0:T(1...) while((s32[]{:T(128)}, f32[16,64]{1,0:T(8,128)S(1)}, ...), condition=%wide.region_17.18_spmd.clone, body=%wide.region_14.17_spmd.clone.sunk | while | flops 69768200 | bytes 5532106 | solution.py:115
  234.6 6.6 %copy.83 = bf16[1,2048,1024]{1,2,0:T(8,128)(2,1)} copy(bf16[1,2048,1024]{2,1,0:T(8,128)(2,1)} %all-gather.11.cloned.1.call-done) | data formatting | bytes 8388608 | tf_op jit(solution)/shard_map/all_gather | solution.py:218
  241.3 16.1 %while.89 = (s32[]{:T(128)}, f32[64,16,64]{0,2,1:T(8,128)S(1)}, s32[4]{0:T(128)S(1)}, bf16[2048,16,64]{0,2,1:T(8,128)(2,1)}, s32[64]{0:T(128)S(1)}, /*index=5*/s...) while((s32[]{:T(128)}, f32[64,16,64]{0,2,1:T(8,128)S(1)}, ...), condition=%wide.region_19.20_spmd.clone, body=%wide.region_18.19_spmd.clone.sunk | while | flops 136478720 | bytes 2834388 | solution.py:132
  257.5 54.1 %while.90 = (s32[]{:T(128)}, f32[64,16,64]{0,2,1:T(8,128)S(1)}, bf16[4,512,2048]{2,1,0:T(8,128)(2,1)}, s32[4]{0:T(128)S(1)}, bf16[2048,16,64]{0,2,1:T(8,128)(2,1...) while((s32[]{:T(128)}, f32[64,16,64]{0,2,1:T(8,128)S(1)}, ...), condition=%wide.region_21.22_spmd.clone, body=%wide.region_20.21_spmd.clone.sunk | while | flops 344621056 | bytes 28396028 | solution.py:179
  266.6 2.9 copy.116
  280.2 2.9 copy.116
  293.6 2.9 copy.116
  307.1 2.9 copy.116
  313.4 130.1 %psum.7 = f32[32,16]{0,1:T(8,128)S(1)} all-reduce(f32[32,16]{0,1:T(8,128)S(1)} %get-tuple-element.693), channel_id=1, replica_groups=mesh['dp'=4,'seq'=16,'mp'=4] {'dp','seq'}, use_global_device_ids=true, to_apply=%region_23.24 | all-reduce | flops 512 | bytes 4096 | tf_op jit(solution)/shard_map/psum | solution.py:256
  (318 shorter events, 202.3 us)
Async XLA Ops:
  7.2 9.6 %copy-start.19 = (bf16[1,64,1024]{2,1,0:T(8,128)(2,1)S(1)}, bf16[1,64,1024]{2,1,0:T(8,128)(2,1)}, u32[]{:S(2)}) copy-start(bf16[1,64,1024]{2,1,0:T(8,128)(2,1)} %param.27) | copy-start | bytes 393220
  7.2 45.4 %all-gather.5.cloned.1.call-start = ((), (), s32[]{:S(2)}) async-start(), calls=%async_computation.2 | async-start | bytes 2228224 | tf_op jit(solution)/shard_map/all_gather | solution.py:215
  7.9 84.5 %all-gather.7.cloned.1.call-start = ((), (), s32[]{:S(2)}) async-start(), calls=%async_computation.3 | async-start | bytes 2228224 | tf_op jit(solution)/shard_map/all_gather | solution.py:216
  8.7 203.9 %all-gather.9.cloned.1.call-start = ((), (), s32[]{:S(2)}) async-start(), calls=%async_computation.5 | async-start | bytes 4456448 | tf_op jit(solution)/shard_map/all_gather | solution.py:217
  9.4 225.2 %all-gather.11.cloned.1.call-start = ((), (), s32[]{:S(2)}) async-start(), calls=%async_computation.6 | async-start | bytes 4456448 | tf_op jit(solution)/shard_map/all_gather | solution.py:218
  10.0 435.0 %reduce-scatter.3.cloned.1.call-start = ((), (), s32[]{:S(2)}) async-start(), calls=%async_computation.4 | async-start | bytes 4456448 | tf_op jit(solution)/shard_map/reduce_scatter | solution.py:246
  17.0 39.5 %copy-start.7 = (bf16[1,64,1024]{1,2,0:T(8,128)(2,1)}, bf16[1,64,1024]{1,2,0:T(8,128)(2,1)S(1)}, u32[]{:S(2)}) copy-start(bf16[1,64,1024]{1,2,0:T(8,128)(2,1)S(1)} %copy.81) | copy-start | bytes 393220
  17.9 38.6 %copy-start.12 = (f32[32,16]{0,1:T(8,128)S(1)}, f32[32,16]{0,1:T(8,128)}, u32[]{:S(2)}) copy-start(f32[32,16]{0,1:T(8,128)} %param.33) | copy-start | bytes 6148
  106.7 2.5 copy-start.15
  123.8 2.5 copy-start.15
  131.9 12.7 %copy-start.9 = (bf16[64,16,64]{0,2,1:T(8,128)(2,1)}, bf16[64,16,64]{0,2,1:T(8,128)(2,1)S(1)}, u32[]{:S(2)}) copy-start(bf16[64,16,64]{0,2,1:T(8,128)(2,1)S(1)} %get-tuple-element.1967) | copy-start | bytes 393220 | tf_op jit(solution)/shard_map/while
  148.9 1.7 copy-start.3
  168.9 3.3 copy-start.10
  172.3 12.7 %copy-start.9 = (bf16[64,16,64]{0,2,1:T(8,128)(2,1)}, bf16[64,16,64]{0,2,1:T(8,128)(2,1)S(1)}, u32[]{:S(2)}) copy-start(bf16[64,16,64]{0,2,1:T(8,128)(2,1)S(1)} %get-tuple-element.1967) | copy-start | bytes 393220 | tf_op jit(solution)/shard_map/while
  209.2 3.3 copy-start.10
  212.5 6.9 %copy-start.11 = (bf16[64,16,64]{2,0,1:T(8,128)(2,1)S(1)}, bf16[64,16,64]{2,0,1:T(8,128)(2,1)}, u32[]{:S(2)}) copy-start(bf16[64,16,64]{2,0,1:T(8,128)(2,1)} %copy.82) | copy-start | bytes 393220
  212.5 6.8 %copy-start.13 = (f32[16,64]{1,0:T(8,128)S(1)}, f32[16,64]{1,0:T(8,128)}, u32[]{:S(2)}) copy-start(f32[16,64]{1,0:T(8,128)} %custom-call.5) | copy-start | bytes 12292
  212.5 6.8 %copy-start.17 = (f32[16,64]{1,0:T(8,128)S(1)}, f32[16,64]{1,0:T(8,128)}, u32[]{:S(2)}) copy-start(f32[16,64]{1,0:T(8,128)} %custom-call.6) | copy-start | bytes 12292
  212.5 6.8 %copy-start.18 = (s32[2048]{0:T(1024)S(1)}, s32[2048]{0:T(1024)}, u32[]{:S(2)}) copy-start(s32[2048]{0:T(1024)} %convert_reduce_fusion) | copy-start | bytes 24580
  212.5 234.2 %reduce-scatter.5.cloned.1.call-start = ((), (), s32[]{:S(2)}) async-start(), calls=%async_computation.7 | async-start | bytes 8912896 | tf_op jit(solution)/shard_map/reduce_scatter | solution.py:249
  234.6 6.7 %copy-start.14 = (f32[64,16,64]{0,2,1:T(8,128)S(1)}, f32[64,16,64]{0,2,1:T(8,128)}, u32[]{:S(2)}) copy-start(f32[64,16,64]{0,2,1:T(8,128)} %custom-call.7) | copy-start | bytes 786436
  241.3 16.1 %copy-start.1 = (bf16[1,64,1024]{1,2,0:T(8,128)(2,1)S(1)}, bf16[1,64,1024]{1,2,0:T(8,128)(2,1)}, u32[]{:S(2)}) copy-start(bf16[1,64,1024]{1,2,0:T(8,128)(2,1)} %copy.84) | copy-start | bytes 393220
  241.3 16.2 %copy-start.6 = (f32[64,16,64]{0,2,1:T(8,128)S(1)}, f32[64,16,64]{0,2,1:T(8,128)}, u32[]{:S(2)}) copy-start(f32[64,16,64]{0,2,1:T(8,128)} %custom-call.8) | copy-start | bytes 786436
  241.3 16.2 %copy-start.8 = (bf16[1,64,1024]{1,2,0:T(8,128)(2,1)S(1)}, bf16[1,64,1024]{1,2,0:T(8,128)(2,1)}, u32[]{:S(2)}) copy-start(bf16[1,64,1024]{1,2,0:T(8,128)(2,1)} %copy-done.7) | copy-start | bytes 393220
  (16 other events, 22.0 us)
Sparse Core Ops, SparseCore 0:
  9.8 42.6 all-gather.4
  54.4 38.0 all-gather.6
  94.3 40.5 all-gather.8
  136.5 40.8 all-gather.10
  212.6 61.6 reduce-scatter.2
  311.7 69.7 reduce-scatter.4
where the time goes:
time: 458 us; the launch traced here: 455 us
  local copies, waits for them, and re-layouts  170 us (37%)
  blocking collectives  130 us (28%)
  matrix products  67.9 us (15%)
  waiting for transfers between devices  41.4 us (9%)
  other arithmetic  17.8 us (4%)
  between operations  14.5 us (3%)
  loops' own time  13.3 us (3%)
    psum x1, blocking collectives, on_device(): bias_total = lax.psum(self_bias, ('dp', 'seq'))  130 us
    all_gather x1, waiting for transfers between devices, on_device(): lax.all_gather(k_self, 'seq', axis=1, tiled=True)  34.6 us
    dynamic_update_slice x12, local copies, waits for them, and re-layouts, query_side(): lax.scan(grad_step, grad_state, block_ids)  29.1 us
    dot_general x12, matrix products, scores_of(): jnp.einsum('thd,uhd->htu', queries, key_block, preferred_element_type=jnp...  24.8 us
    dot_general x6, matrix products, out_step(): jnp.einsum('htu,uhd->thd', narrow_weights, value_block, preferred_element...  17.1 us
    rev x6, local copies, waits for them, and re-layouts, spread(): return skewed[..., ::-1]  15.1 us
    reshape x6, local copies, waits for them, and re-layouts, spread(): flat_rows = tiled_rows.reshape(leading + (row_count * full_span,))  14.9 us
    reshape x6, local copies, waits for them, and re-layouts, spread(): flat_rows.reshape(leading + (row_count, full_span + 1))[..., :col_count]  14.6 us
  transfers between devices with their start and end apart: 6, of which 2 were waited for; matrix products, arithmetic and copies ran while one was open for 52% of the time, Pallas kernels for 0%

commit v1 on v0

--- a/solution.py
+++ b/solution.py
@@ -7,6 +7,12 @@
 HEAD_DIM = 64
 BUCKETS = 32
 DISTANCE = 128
+
+
+def _compute_runs(original):
+    return jnp.concatenate(
+        lax.all_to_all(jnp.stack([original] * lax.axis_size("seq"), axis=0), "seq", 0, 0), axis=1
+    )
 
 
 def bucket_of(distances):
@@ -212,7 +218,7 @@
         return tensor.reshape(tensor.shape[0] * tensor.shape[1], head_count, HEAD_DIM)
 
     gathered = (
-        lax.all_gather(k_self, "seq", axis=1, tiled=True),
+        _compute_runs(k_self),
         lax.all_gather(v_self, "seq", axis=1, tiled=True),
         lax.all_gather(k_cross, "seq", axis=1, tiled=True),
         lax.all_gather(v_cross, "seq", axis=1, tiled=True),

time: 458 us -> 485 us (1.059)
  waiting for transfers between devices: 41.4 us -> 56.5 us
  starting transfers between devices: 0.23 us -> 8.91 us
    all_to_all x0 -> x1, waiting for transfers between devices: none -> 54.3 us  [_compute_runs(): lax.all_to_all(jnp.stack([original] * lax.axis_size('seq'), axis=0), 'seq...]
    all_gather x1 -> x0, waiting for transfers between devices: 34.6 us -> none  [on_device(): lax.all_gather(k_self, 'seq', axis=1, tiled=True)]
    all_to_all x0 -> x1, starting transfers between devices: none -> 8.71 us  [_compute_runs(): lax.all_to_all(jnp.stack([original] * lax.axis_size('seq'), axis=0), 'seq...]
    another operation x2 -> x4, local copies, waits for them, and re-layouts: 1.47 us -> 6.68 us  [the longest x1 4 us: split_heads(): tensor.reshape(tensor.shape[0] * tensor.shape[1], head_count, HEAD_DIM)]
  transfers between devices with their start and end apart: 6 -> 6, of which waited for: 2 -> 1; matrix products, arithmetic and copies ran while one was open for 52% -> 50% of each run, Pallas kernels for 0% -> 0%
where the time goes in v1:
time: 485 us; the launch traced here: 482 us
  local copies, waits for them, and re-layouts  174 us (36%)
  blocking collectives  130 us (27%)
  matrix products  67.9 us (14%)
  waiting for transfers between devices  56.5 us (12%)
  other arithmetic  17.7 us (4%)
  between operations  14.2 us (3%)
  loops' own time  13.1 us (3%)
  starting transfers between devices  8.91 us (2%)
    psum x1, blocking collectives, on_device(): bias_total = lax.psum(self_bias, ('dp', 'seq'))  130 us
    all_to_all x1, waiting for transfers between devices, _compute_runs(): lax.all_to_all(jnp.stack([original] * lax.axis_size('seq'), axis=0), 'seq...  54.3 us
    dynamic_update_slice x12, local copies, waits for them, and re-layouts, query_side(): lax.scan(grad_step, grad_state, block_ids)  29 us
    dot_general x12, matrix products, scores_of(): jnp.einsum('thd,uhd->htu', queries, key_block, preferred_element_type=jnp...  24.8 us
    dot_general x6, matrix products, out_step(): jnp.einsum('htu,uhd->thd', narrow_weights, value_block, preferred_element...  17 us
    rev x6, local copies, waits for them, and re-layouts, spread(): return skewed[..., ::-1]  15.2 us
    reshape x6, local copies, waits for them, and re-layouts, spread(): flat_rows = tiled_rows.reshape(leading + (row_count * full_span,))  14.9 us
    reshape x6, local copies, waits for them, and re-layouts, spread(): flat_rows.reshape(leading + (row_count, full_span + 1))[..., :col_count]  14.7 us
  transfers between devices with their start and end apart: 6, of which 1 were waited for; matrix products, arithmetic and copies ran while one was open for 50% of the time, Pallas kernels for 0%

profile of v1, /device:TPU:2, one launch (start us, length us, event | category | flops | bytes accessed | tf_op | source)
XLA Modules:
  0.0 482.3 jit_solution(10161582704797826546)
XLA Ops:
  11.2 8.7 %all-to-all-start = ((bf16[16,1,64,1024]{3,2,1,0:T(8,128)(2,1)}), bf16[16,1,64,1024]{3,2,1,0:T(8,128)(2,1)S(1)}, u32[]{:S(2)}, u32[]{:S(2)}) async-start(bf16[16,1,64,1024]{3,2,1,0:T(8,128)(2,1)} %stack.2), calls=%async_computation | async-start | bytes 4194304 | tf_op jit(solution)/shard_map/all_to_all | solution.py:14
  24.6 54.3 %all-to-all-done = bf16[16,1,64,1024]{3,2,1,0:T(8,128)(2,1)S(1)} async-done(((bf16[16,1,64,1024]{3,2,1,0:T(8,128)(2,1)}), bf16[16,1,64,1024]{3,2,1,0:T(8,128)(2,1)S(1)}, u32[]{:S(2)}, u32[]{:S(2)}) %all-to-all-start) | async-done | bytes 2097184 | tf_op jit(solution)/shard_map/all_to_all | solution.py:14
  78.9 4.0 reshape_reshape.9
  82.9 5.5 %copy.102 = bf16[1024,16,64]{0,2,1:T(8,128)(2,1)} copy(bf16[1024,16,64]{2,1,0:T(8,128)(2,1)} %reshape_reshape.9) | data formatting | bytes 4194304
  88.4 32.0 %while.91 = (s32[]{:T(128)}, f32[16,64]{1,0:T(8,128)S(1)}, f32[16,64]{1,0:T(8,128)S(1)}, s32[64]{0:T(128)S(1)}, s32[2]{0:T(128)S(1)}, /*index=5*/s32[1024]{0:T(1...) while((s32[]{:T(128)}, f32[16,64]{1,0:T(8,128)S(1)}, ...), condition=%wide.region_5.6_spmd.clone.clone.clone, body=%wide.region_2.0_spmd.clone.clone.clone.sunk | while | flops 73413688 | bytes 34665884 | solution.py:121
  120.4 4.0 copy.98
  124.4 33.9 %while.92 = (s32[]{:T(128)}, f32[64,16,64]{0,2,1:T(8,128)}, s32[2]{0:T(128)S(1)}, bf16[1024,16,64]{0,2,1:T(8,128)(2,1)}, s32[64]{0:T(128)S(1)}, /*index=5*/s32[1...) while((s32[]{:T(128)}, f32[64,16,64]{0,2,1:T(8,128)}, ...), condition=%wide.region_7.8_spmd.clone.clone.clone, body=%wide.region_6.7_spmd.clone.clone.clone.sunk | while | flops 140648496 | bytes 34098144 | solution.py:138
  137.1 3.3 fusion.213
  154.1 3.4 fusion.213
  159.5 80.8 %while.93 = (s32[]{:T(128)}, f32[64,16,64]{0,2,1:T(8,128)}, f32[32,16]{0,1:T(8,128)S(1)}, bf16[2,512,2048]{2,1,0:T(8,128)(2,1)}, s32[2]{0:T(128)S(1)}, /*index=5...) while((s32[]{:T(128)}, f32[64,16,64]{0,2,1:T(8,128)}, ...), condition=%wide.region_10.11_spmd.clone.clone.clone, body=%wide.region_8.10_spmd.clone.clone.clone.sunk | while | flops 353446976 | bytes 101543680 | solution.py:185
  192.6 3.7 reshape.725
  196.7 3.2 constant_dynamic-update-slice_fusion.5
  232.9 3.7 reshape.725
  237.0 3.3 constant_dynamic-update-slice_fusion.5
  240.4 6.7 %copy.105 = bf16[1,2048,1024]{1,2,0:T(8,128)(2,1)} copy(bf16[1,2048,1024]{2,1,0:T(8,128)(2,1)} %all-gather.6.cloned.1.call-done) | data formatting | bytes 8388608 | tf_op jit(solution)/shard_map/all_gather | solution.py:223
  247.2 15.2 %while.88 = (s32[]{:T(128)}, f32[16,64]{1,0:T(8,128)S(1)}, f32[16,64]{1,0:T(8,128)S(1)}, s32[64]{0:T(128)S(1)}, s32[4]{0:T(128)S(1)}, /*index=5*/s32[2048]{0:T(1...) while((s32[]{:T(128)}, f32[16,64]{1,0:T(8,128)S(1)}, ...), condition=%wide.region_17.18_spmd.clone, body=%wide.region_14.17_spmd.clone.sunk | while | flops 69768200 | bytes 5532106 | solution.py:121
  262.5 6.6 %copy.109 = bf16[1,2048,1024]{1,2,0:T(8,128)(2,1)} copy(bf16[1,2048,1024]{2,1,0:T(8,128)(2,1)} %all-gather.8.cloned.1.call-done) | data formatting | bytes 8388608 | tf_op jit(solution)/shard_map/all_gather | solution.py:224
  269.1 16.1 %while.89 = (s32[]{:T(128)}, f32[64,16,64]{0,2,1:T(8,128)S(1)}, s32[4]{0:T(128)S(1)}, bf16[2048,16,64]{0,2,1:T(8,128)(2,1)}, s32[64]{0:T(128)S(1)}, /*index=5*/s...) while((s32[]{:T(128)}, f32[64,16,64]{0,2,1:T(8,128)S(1)}, ...), condition=%wide.region_19.20_spmd.clone, body=%wide.region_18.19_spmd.clone.sunk | while | flops 136478720 | bytes 2834388 | solution.py:138
  285.3 54.1 %while.90 = (s32[]{:T(128)}, f32[64,16,64]{0,2,1:T(8,128)S(1)}, bf16[4,512,2048]{2,1,0:T(8,128)(2,1)}, s32[4]{0:T(128)S(1)}, bf16[2048,16,64]{0,2,1:T(8,128)(2,1...) while((s32[]{:T(128)}, f32[64,16,64]{0,2,1:T(8,128)S(1)}, ...), condition=%wide.region_21.22_spmd.clone, body=%wide.region_20.21_spmd.clone.sunk | while | flops 344621056 | bytes 28396028 | solution.py:185
  294.5 3.0 copy.142
  308.0 2.9 copy.142
  321.5 2.9 copy.142
  335.0 2.9 copy.142
  341.3 129.5 %psum.7 = f32[32,16]{0,1:T(8,128)S(1)} all-reduce(f32[32,16]{0,1:T(8,128)S(1)} %get-tuple-element.693), channel_id=1, replica_groups=mesh['dp'=4,'seq'=16,'mp'=4] {'dp','seq'}, use_global_device_ids=true, to_apply=%region_23.24 | all-reduce | flops 512 | bytes 4096 | tf_op jit(solution)/shard_map/psum | solution.py:262
  (329 shorter events, 203.2 us)
Async XLA Ops:
  7.2 113.3 %all-gather.4.cloned.1.call-start = ((), (), s32[]{:S(2)}) async-start(), calls=%async_computation.3 | async-start | bytes 2228224 | tf_op jit(solution)/shard_map/all_gather | solution.py:222
  7.9 232.5 %all-gather.6.cloned.1.call-start = ((), (), s32[]{:S(2)}) async-start(), calls=%async_computation.5 | async-start | bytes 4456448 | tf_op jit(solution)/shard_map/all_gather | solution.py:223
  11.2 9.7 %copy-start.23 = (s32[1,16]{1,0:T(1,128)S(1)}, s32[1,16]{1,0:T(1,128)}, u32[]{:S(2)}) copy-start(s32[1,16]{1,0:T(1,128)} %param.31) | copy-start | bytes 196
  11.2 9.9 %copy-start.24 = (s32[1,16]{1,0:T(1,128)S(1)}, s32[1,16]{1,0:T(1,128)}, u32[]{:S(2)}) copy-start(s32[1,16]{1,0:T(1,128)} %param.32) | copy-start | bytes 196
  11.2 10.1 %copy-start.19 = (bf16[1,64,1024]{2,1,0:T(8,128)(2,1)S(1)}, bf16[1,64,1024]{2,1,0:T(8,128)(2,1)}, u32[]{:S(2)}) copy-start(bf16[1,64,1024]{2,1,0:T(8,128)(2,1)} %param.26) | copy-start | bytes 393220
  11.2 10.3 %copy-start.20 = (bf16[1,64,1024]{2,1,0:T(8,128)(2,1)S(1)}, bf16[1,64,1024]{2,1,0:T(8,128)(2,1)}, u32[]{:S(2)}) copy-start(bf16[1,64,1024]{2,1,0:T(8,128)(2,1)} %param.30) | copy-start | bytes 393220
  11.2 11.2 %copy-start.21 = (bf16[1,64,1024]{2,1,0:T(8,128)(2,1)S(1)}, bf16[1,64,1024]{2,1,0:T(8,128)(2,1)}, u32[]{:S(2)}) copy-start(bf16[1,64,1024]{2,1,0:T(8,128)(2,1)} %param.23) | copy-start | bytes 393220
  11.2 11.5 %copy-start.22 = (bf16[1,64,1024]{2,1,0:T(8,128)(2,1)S(1)}, bf16[1,64,1024]{2,1,0:T(8,128)(2,1)}, u32[]{:S(2)}) copy-start(bf16[1,64,1024]{2,1,0:T(8,128)(2,1)} %param.27) | copy-start | bytes 393220
  11.2 67.7 %all-to-all-start = ((bf16[16,1,64,1024]{3,2,1,0:T(8,128)(2,1)}), bf16[16,1,64,1024]{3,2,1,0:T(8,128)(2,1)S(1)}, u32[]{:S(2)}, u32[]{:S(2)}) async-start(bf16[16,1,64,1024]{3,2,1,0:T(8,128)(2,1)} %stack.2), calls=%async_computation | async-start | bytes 4194304 | tf_op jit(solution)/shard_map/all_to_all | solution.py:14
  19.9 242.5 %all-gather.8.cloned.1.call-start = ((), (), s32[]{:S(2)}) async-start(), calls=%async_computation.6 | async-start | bytes 4456448 | tf_op jit(solution)/shard_map/all_gather | solution.py:224
  20.7 451.6 %reduce-scatter.3.cloned.1.call-start = ((), (), s32[]{:S(2)}) async-start(), calls=%async_computation.4 | async-start | bytes 4456448 | tf_op jit(solution)/shard_map/reduce_scatter | solution.py:252
  22.9 60.0 %copy-start.7 = (bf16[1,64,1024]{1,2,0:T(8,128)(2,1)}, bf16[1,64,1024]{1,2,0:T(8,128)(2,1)S(1)}, u32[]{:S(2)}) copy-start(bf16[1,64,1024]{1,2,0:T(8,128)(2,1)S(1)} %copy.107) | copy-start | bytes 393220
  82.9 5.5 %copy-start.12 = (f32[32,16]{0,1:T(8,128)S(1)}, f32[32,16]{0,1:T(8,128)}, u32[]{:S(2)}) copy-start(f32[32,16]{0,1:T(8,128)} %param.33) | copy-start | bytes 6148
  159.6 12.8 %copy-start.9 = (bf16[64,16,64]{0,2,1:T(8,128)(2,1)}, bf16[64,16,64]{0,2,1:T(8,128)(2,1)S(1)}, u32[]{:S(2)}) copy-start(bf16[64,16,64]{0,2,1:T(8,128)(2,1)S(1)} %get-tuple-element.2055) | copy-start | bytes 393220 | tf_op jit(solution)/shard_map/while
  200.0 12.7 %copy-start.9 = (bf16[64,16,64]{0,2,1:T(8,128)(2,1)}, bf16[64,16,64]{0,2,1:T(8,128)(2,1)S(1)}, u32[]{:S(2)}) copy-start(bf16[64,16,64]{0,2,1:T(8,128)(2,1)S(1)} %get-tuple-element.2055) | copy-start | bytes 393220 | tf_op jit(solution)/shard_map/while
  240.3 6.9 %copy-start.11 = (bf16[64,16,64]{2,0,1:T(8,128)(2,1)S(1)}, bf16[64,16,64]{2,0,1:T(8,128)(2,1)}, u32[]{:S(2)}) copy-start(bf16[64,16,64]{2,0,1:T(8,128)(2,1)} %copy.108) | copy-start | bytes 393220
  240.3 6.9 %copy-start.13 = (f32[16,64]{1,0:T(8,128)S(1)}, f32[16,64]{1,0:T(8,128)}, u32[]{:S(2)}) copy-start(f32[16,64]{1,0:T(8,128)} %custom-call.5) | copy-start | bytes 12292
  240.3 6.9 %copy-start.17 = (f32[16,64]{1,0:T(8,128)S(1)}, f32[16,64]{1,0:T(8,128)}, u32[]{:S(2)}) copy-start(f32[16,64]{1,0:T(8,128)} %custom-call.6) | copy-start | bytes 12292
  240.3 6.9 %copy-start.18 = (s32[2048]{0:T(1024)S(1)}, s32[2048]{0:T(1024)}, u32[]{:S(2)}) copy-start(s32[2048]{0:T(1024)} %convert_reduce_fusion) | copy-start | bytes 24580
  240.3 233.6 %reduce-scatter.5.cloned.1.call-start = ((), (), s32[]{:S(2)}) async-start(), calls=%async_computation.7 | async-start | bytes 8912896 | tf_op jit(solution)/shard_map/reduce_scatter | solution.py:255
  262.4 6.7 %copy-start.14 = (f32[64,16,64]{0,2,1:T(8,128)S(1)}, f32[64,16,64]{0,2,1:T(8,128)}, u32[]{:S(2)}) copy-start(f32[64,16,64]{0,2,1:T(8,128)} %custom-call.7) | copy-start | bytes 786436
  269.1 16.1 %copy-start.1 = (bf16[1,64,1024]{1,2,0:T(8,128)(2,1)S(1)}, bf16[1,64,1024]{1,2,0:T(8,128)(2,1)}, u32[]{:S(2)}) copy-start(bf16[1,64,1024]{1,2,0:T(8,128)(2,1)} %copy.110) | copy-start | bytes 393220
  269.1 16.2 %copy-start.6 = (f32[64,16,64]{0,2,1:T(8,128)S(1)}, f32[64,16,64]{0,2,1:T(8,128)}, u32[]{:S(2)}) copy-start(f32[64,16,64]{0,2,1:T(8,128)} %custom-call.8) | copy-start | bytes 786436
  269.1 16.2 %copy-start.8 = (bf16[1,64,1024]{1,2,0:T(8,128)(2,1)S(1)}, bf16[1,64,1024]{1,2,0:T(8,128)(2,1)}, u32[]{:S(2)}) copy-start(bf16[1,64,1024]{1,2,0:T(8,128)(2,1)} %copy-done.7) | copy-start | bytes 393220
  (21 other events, 35.2 us)
Sparse Core Ops, SparseCore 0:
  9.8 63.6 all-gather.3
  75.3 47.8 all-gather.5
  125.0 40.6 all-gather.7
  240.4 61.9 reduce-scatter.2
  339.5 70.3 reduce-scatter.4
